TPU v7x, 256 devices: a whole 4x4x8 slice. The times are simulated.
256 devices in a mesh: blk: 32 (over z, y_lo, core), head: 8 (over y_hi, x).
Axes of the slice: x: 4, y: 4 (y_hi: 2, y_lo: 2; y = y_hi * 2 + y_lo), z: 8, core: 2. Of those that a mesh axis runs over, the one named last changes fastest.
Arguments:
- hidden: bfloat16 [2048, 5120], P('blk'), may hold values from -6 to 6
- norm_gain: float32 [5120], replicated, may hold values from 0.1 to 1.9
- w_query: bfloat16 [5120, 5120], P('blk', 'head'), may hold values from -0.078125 to 0.078125
- key_projection_weight: bfloat16 [5120, 1024], P('blk', 'head'), may hold values from -0.3125 to 0.3125
- value_projection_weight: bfloat16 [5120, 1024], P('blk', 'head'), may hold values from -0.078125 to 0.078125
- w_out: bfloat16 [5120, 5120], P('head', 'blk'), may hold values from -0.078125 to 0.078125
- cache_keys: bfloat16 [8, 65536, 128], P('head', 'blk'), may hold values from -1024 to 1024
- earlier_values: bfloat16 [8, 65536, 128], P('head', 'blk'), may hold values from -6 to 6
- cache_len: int32 [32], P('blk'), may hold values from 512 to 2048, as said below
- stretch_start: int32 [1], replicated, may hold values from 0 to 4194303
Outputs:
- attention_out: bfloat16 [2048, 5120], P('head', 'blk')
Inputs may be any that keep to these rules, and one draw needn't show every extreme that they name: Cache shard s holds valid entries at its first cache_len[s] positions, the rest are ignored; at least one shard is full.
All inputs are finite; a program needn't handle non-finite values.
Results may differ from a plain program's by a relative error of at most 0.023.
The roundings to bfloat16 on the way count: a program that leaves them out, or rounds other values in their place, can miss the bound.
Values may be sent and summed in bfloat16 or wider, within the bound.
No kernel may reach another device: no remote copies, remote signals or barrier semaphores. Data moves between devices by JAX's collectives and lax.ppermute only.
A program may use at most 192 MiB of HBM per device.

v0:
```python
import math

import jax
import jax.numpy as jnp
from jax import lax
from jax.sharding import Mesh
from jax.sharding import PartitionSpec as P

BLK = ("blk_0", "blk_1", "blk_2")


neg_large = -1e30


def sent_together(arrays, axis, dim, along):
    widths = [a.shape[along] for a in arrays]
    both = jnp.concatenate(arrays, axis=along)
    whole = lax.all_gather(both, axis, axis=dim, tiled=True)
    return tuple(jnp.split(whole, [sum(widths[:k]) for k in range(1, len(widths))], axis=along))


def copy_for_each(x, axis):
    size = lax.axis_size(axis)
    return lax.all_to_all(jnp.broadcast_to(x[None], (size, *x.shape)), axis, 0, 0, tiled=True)


def laid_out(parts, dim):
    parts = jnp.moveaxis(parts, 0, dim)
    lengths = parts.shape
    return parts.reshape(*lengths[:dim], lengths[dim] * lengths[dim + 1], *lengths[dim + 2 :])


def gather_axes(x, axes, dim):
    far, near = axes
    parts = copy_for_each(copy_for_each(x, far), near)
    return laid_out(parts.swapaxes(0, 1).reshape(-1, *x.shape), dim)


def taken_together(x, axis):
    everything = copy_for_each(x, axis)
    return jnp.max(everything, axis=0)


def split_up(x, dim, size):
    before, after = (x.shape[:dim], x.shape[dim + 1 :])
    return jnp.moveaxis(x.reshape(*before, size, -1, *after), dim, 0)


def summed_on_arrival(x, axis, dim):
    size = lax.axis_size(axis)
    parts = lax.all_to_all(split_up(x, dim, size), axis, 0, 0, tiled=True)
    return jnp.sum(parts.astype(jnp.float32), axis=0)


def sum_by_axis(x, axes, dim):
    far, near = axes
    parts = split_up(x, dim, lax.axis_size(far))
    nearer = summed_on_arrival(parts, near, dim + 1)
    arrived = lax.all_to_all(
        nearer.astype(jnp.bfloat16), far, split_axis=0, concat_axis=0, tiled=True
    )
    return arrived.astype(jnp.float32).sum(axis=0)


def sent_together_2(arrays, axis, dim, along):
    both = jnp.concatenate(arrays, axis=along)
    whole, at, outs = (sum_by_axis(both, axis, dim), 0, [])
    for a in arrays:
        outs.append(lax.slice_in_dim(whole, at, at + a.shape[along], axis=along))
        at += a.shape[along]
    return tuple(outs)


def block_stats(queries, key_block, value_block, key_mask):
    scores = jnp.einsum("rkgd,kjd->rkgj", queries, key_block, preferred_element_type=jnp.float32)
    scores = jnp.where(key_mask, scores, neg_large)
    maximum = jnp.max(scores, axis=-1)
    weights = jnp.where(key_mask, jnp.exp(scores - maximum[..., None]), 0.0)
    denominator = jnp.sum(weights, axis=-1)
    numerator = jnp.einsum(
        "rkgj,kjd->rkgd",
        weights.astype(jnp.bfloat16),
        value_block,
        preferred_element_type=jnp.float32,
    )
    return (maximum, denominator, numerator)


def combine(first, second):
    max_one, den_one, num_one = first
    max_two, den_two, num_two = second
    maximum = jnp.maximum(max_one, max_two)
    scale_one = jnp.exp(max_one - maximum)
    scale_two = jnp.exp(max_two - maximum)
    return (
        maximum,
        den_one * scale_one + den_two * scale_two,
        num_one * scale_one[..., None] + num_two * scale_two[..., None],
    )


def cache_pass(queries, cache_keys, earlier_values, length):
    cache_rows = cache_keys.shape[1]
    block_len = math.gcd(cache_rows, 1024)
    lead_shape = queries.shape[:3]
    initial = (
        jnp.full(lead_shape, neg_large, jnp.float32),
        jnp.zeros(lead_shape, jnp.float32),
        jnp.zeros(queries.shape, jnp.float32),
    )

    def visit(block_index, running):
        first_key = block_index * block_len
        key_block = lax.dynamic_slice_in_dim(cache_keys, first_key, block_len, 1)
        value_block = lax.dynamic_slice_in_dim(earlier_values, first_key, block_len, 1)
        key_mask = (first_key + jnp.arange(block_len, dtype=jnp.int32) < length)[
            None, None, None, :
        ]
        return combine(running, block_stats(queries, key_block, value_block, key_mask))

    return lax.fori_loop(0, cache_rows // block_len, visit, initial)


def per_device(
    hidden,
    norm_gain,
    w_query,
    key_projection_weight,
    value_projection_weight,
    w_out,
    cache_keys,
    earlier_values,
    cache_len,
    stretch_start,
):
    row_count, model_width = hidden.shape
    kv_local, cache_rows, head_dim = cache_keys.shape
    q_cols = w_query.shape[1]
    heads_local = q_cols // head_dim
    query_group_count = heads_local // kv_local
    stream = hidden.astype(jnp.float32)
    normed = (
        stream * lax.rsqrt(jnp.mean(stream * stream, axis=-1, keepdims=True) + 1e-05) * norm_gain
    ).astype(jnp.bfloat16)
    pieces = sent_together((w_query, key_projection_weight, value_projection_weight), BLK, 0, 1)
    query_sum, key_sum, value_sum = tuple(
        (jnp.dot(normed, w_piece, preferred_element_type=jnp.float32) for w_piece in pieces)
    )
    queries = query_sum.astype(jnp.bfloat16)
    fresh_keys = key_sum.astype(jnp.bfloat16)
    fresh_values = value_sum.astype(jnp.bfloat16)
    start_row = lax.axis_index(BLK) * row_count
    token_index = start_row + jnp.arange(row_count, dtype=jnp.int32)
    positions = stretch_start[0] + token_index
    temper = jnp.log(((positions + 1) // 8192).astype(jnp.float32) + 1.0) * 0.1 + 1.0
    scaled_scores = (
        lax.optimization_barrier(queries).astype(jnp.float32)
        * (temper * head_dim ** (-0.5))[:, None]
    ).astype(jnp.bfloat16)
    local_queries = scaled_scores.reshape(row_count, kv_local, query_group_count, head_dim)
    span_keys, span_values = sent_together((fresh_keys, fresh_values), BLK, 0, 1)
    stretch_total = span_keys.shape[0]
    span_keys = span_keys.reshape(stretch_total, kv_local, head_dim).transpose(1, 0, 2)
    span_values = span_values.reshape(stretch_total, kv_local, head_dim).transpose(1, 0, 2)
    causal = (jnp.arange(stretch_total, dtype=jnp.int32)[None, :] <= token_index[:, None])[
        :, None, None, :
    ]
    own_stats = block_stats(local_queries, span_keys, span_values, causal)
    length = cache_len[0]
    all_queries = gather_axes(scaled_scores, (("blk_0", "blk_1"), "blk_2"), 0)
    total_rows = all_queries.shape[0]
    all_queries = all_queries.reshape(total_rows, kv_local, query_group_count, head_dim)
    maxima, denominators, numerators = cache_pass(all_queries, cache_keys, earlier_values, length)
    peak = taken_together(maxima.astype(jnp.bfloat16), BLK).astype(maxima.dtype)
    rescale = jnp.exp(maxima - peak)
    numer_sum, denom_sum = sent_together_2(
        (
            (numerators * rescale[..., None]).reshape(total_rows, q_cols).astype(jnp.bfloat16),
            (denominators * rescale).reshape(total_rows, heads_local).astype(jnp.bfloat16),
        ),
        (("blk_0", "blk_1"), "blk_2"),
        0,
        1,
    )
    own_peak = lax.dynamic_slice_in_dim(peak, start_row, row_count, 0)
    cache_stats = (
        own_peak,
        denom_sum.reshape(row_count, kv_local, query_group_count),
        numer_sum.reshape(row_count, kv_local, query_group_count, head_dim),
    )
    maximum, denominator, numerator = combine(cache_stats, own_stats)
    context = (numerator / denominator[..., None]).astype(jnp.bfloat16).reshape(row_count, q_cols)
    terms = jnp.dot(
        gather_axes(context, (("blk_0", "blk_1"), "blk_2"), 0),
        w_out,
        preferred_element_type=jnp.float32,
    )
    return summed_on_arrival(terms.astype(jnp.bfloat16), "head", 0).astype(jnp.bfloat16)


def solution(mesh):
    finer = Mesh(
        mesh.devices.reshape(8, 2, 2, mesh.shape["head"]), ("blk_0", "blk_1", "blk_2", "head")
    )
    return jax.shard_map(
        per_device,
        mesh=finer,
        in_specs=(
            P(BLK, None),
            P(),
            P(BLK, "head"),
            P(BLK, "head"),
            P(BLK, "head"),
            P("head", BLK),
            P("head", BLK, None),
            P("head", BLK, None),
            P(BLK),
            P(),
        ),
        out_specs=P("head", BLK),
        check_vma=False,
    )
```

profile of v0, /device:TPU:2, one launch (start us, length us, event | category | flops | bytes accessed | tf_op | source)
XLA Modules:
  0.0 436.5 jit_solution(17777066769451128059)
XLA Ops:
  6.5 1.8 pad_maximum_fusion
  10.3 75.1 %all-gather.3.cloned.1.call-done = bf16[5120,896]{1,0:T(8,128)(2,1)} async-done(((bf16[160,896]{1,0:T(8,128)(2,1)}), bf16[5120,896]{1,0:T(8,128)(2,1)}) %all-gather.3.cloned.1.call-update) | async-done | bytes 9175056 | tf_op jit(solution)/shard_map/all_gather | solution.py:18
  85.4 4.4 %fusion.61 = bf16[64,640]{1,0:T(8,128)(2,1)S(1)} fusion(bf16[5120,896]{1,0:T(8,128)(2,1)} %all-gather.3.cloned.1.call-done, bf16[64,5120]{1,0:T(8,128)(2,1)} %param.12, f32[5120]{0:T(1024)} %param.13, f32[64]{0:T(128)S(1)} %add_rsqrt_fusion), kind=kOutput, calls=%fused_computation.65 | convolution fusion | flops 420782080 | bytes 7311616 | tf_op jit(solution)/shard_map/dot_general | solution.py:147
  91.7 5.5 %all-to-all-start = ((bf16[16,64,640]{2,1,0:T(8,128)(2,1)}), bf16[16,64,640]{2,1,0:T(8,128)(2,1)S(1)}, u32[]{:S(2)}, u32[]{:S(2)}) async-start(bf16[16,64,640]{2,1,0:T(8,128)(2,1)} %broadcast_in_dim.122), calls=%async_computation | async-start | bytes 2621440 | tf_op jit(solution)/shard_map/all_to_all | solution.py:24
  97.3 34.7 %all-to-all-done = bf16[16,64,640]{2,1,0:T(8,128)(2,1)S(1)} async-done(((bf16[16,64,640]{2,1,0:T(8,128)(2,1)}), bf16[16,64,640]{2,1,0:T(8,128)(2,1)S(1)}, u32[]{:S(2)}, u32[]{:S(2)}) %all-to-all-start) | async-done | bytes 1310752 | tf_op jit(solution)/shard_map/all_to_all | solution.py:24
  132.3 5.8 %all_to_all.40 = bf16[2,16,64,640]{3,2,1,0:T(8,128)(2,1)S(1)} all-to-all(bf16[2,16,64,640]{3,2,1,0:T(8,128)(2,1)S(1)} %broadcast_in_dim.123), channel_id=1, replica_groups=mesh['blk_0'=8,'blk_1'=2,'blk_2'=2,'head'=8] {'blk_2'}, dimensions={0} | all-to-all | bytes 5242880 | tf_op jit(solution)/shard_map/all_to_all | solution.py:24
  138.4 4.2 reshape_reshape_reshape.3
  142.6 2.6 copy.71
  145.3 111.2 %while.18 = (s32[]{:T(128)}, f32[2048,1,5]{0,2,1:T(8,128)S(1)}, f32[2048,1,5]{0,2,1:T(8,128)S(1)}, f32[2048,1,5,128]{0,3,2,1:T(8,128)}, s32[]{:T(128)}, /*index=...) while((s32[]{:T(128)}, f32[2048,1,5]{0,2,1:T(8,128)S(1)}, ...), condition=%wide.region_4.5_spmd.clone, body=%wide.region_1.4_spmd.clone.sunk | while | flops 5478893568 | bytes 142415088 | solution.py:121
  146.0 16.2 %bitcast_reduce_fusion.2 = (f32[2048,5]{0,1:T(8,128)S(1)}, f32[1024,2048,5]{1,0,2:T(8,128)}) fusion(pred[1024]{0:T(1024)(128)(4,1)S(1)} %add_compare_fusion.2, bf16[2048,1,5,128]{3,0,2,1:T(8,128)(2,1)S(1)} %get-tuple-element.344, bf16[1,2048,128]{2,1,0:T(8,128)(2,1)S(1)} %get-tuple-element.343, s32[]{:T(128)S(6)} %select_n.112), kind=kOutput, calls=%fused_computation.1.clone.1 | convolution fusion | flops 2705315840 | bytes 44868612 | tf_op jit(solution)/shard_map/while/body/eval_jaxpr/rkgd,kjd->rkgj/dot_general | solution.py:75
  162.2 18.4 %fusion.99 = f32[2048,5]{0,1:T(8,128)S(1)} fusion(f32[1024,2048,5]{1,0,2:T(8,128)} %get-tuple-element.310, f32[2048,5]{0,1:T(8,128)S(1)} %get-tuple-element.308, pred[1024]{0:T(1024)(128)(4,1)S(1)} %add_compare_fusion.2), kind=kLoop, calls=%fused_computation.6.clone.1 | loop fusion | flops 41932800 | bytes 42025984 | tf_op jit(solution)/shard_map/while/body/eval_jaxpr/reduce_sum | solution.py:79
  180.7 19.3 %bitcast_add_fusion.2 = f32[2048,1,5,128]{0,3,2,1:T(8,128)} fusion(f32[2048,1,5,128]{0,3,2,1:T(8,128)} %get-tuple-element.329, f32[1024,2048,5]{1,0,2:T(8,128)} %get-tuple-element.310, f32[2048,5]{0,1:T(8,128)S(1)} %get-tuple-element.308, pred[1024]{0:T(1024)(128)(4,1)S(1)} %add_compare_fusion.2, f32[2048,5]{0,1:T(8,128)S(1)} %get-tuple-element.312, ...), kind=kOutput, calls=%fused_computation.11.clone.1 | convolution fusion | flops 2731540480 | bytes 52889604 | tf_op jit(solution)/shard_map/while/body/eval_jaxpr/rkgj,kjd->rkgd/dot_general | solution.py:80
  200.7 16.2 %bitcast_reduce_fusion.2 = (f32[2048,5]{0,1:T(8,128)S(1)}, f32[1024,2048,5]{1,0,2:T(8,128)}) fusion(pred[1024]{0:T(1024)(128)(4,1)S(1)} %add_compare_fusion.2, bf16[2048,1,5,128]{3,0,2,1:T(8,128)(2,1)S(1)} %get-tuple-element.344, bf16[1,2048,128]{2,1,0:T(8,128)(2,1)S(1)} %get-tuple-element.343, s32[]{:T(128)S(6)} %select_n.112), kind=kOutput, calls=%fused_computation.1.clone.1 | convolution fusion | flops 2705315840 | bytes 44868612 | tf_op jit(solution)/shard_map/while/body/eval_jaxpr/rkgd,kjd->rkgj/dot_general | solution.py:75
  216.9 18.4 %fusion.99 = f32[2048,5]{0,1:T(8,128)S(1)} fusion(f32[1024,2048,5]{1,0,2:T(8,128)} %get-tuple-element.310, f32[2048,5]{0,1:T(8,128)S(1)} %get-tuple-element.308, pred[1024]{0:T(1024)(128)(4,1)S(1)} %add_compare_fusion.2), kind=kLoop, calls=%fused_computation.6.clone.1 | loop fusion | flops 41932800 | bytes 42025984 | tf_op jit(solution)/shard_map/while/body/eval_jaxpr/reduce_sum | solution.py:79
  235.4 21.0 %bitcast_add_fusion.2 = f32[2048,1,5,128]{0,3,2,1:T(8,128)} fusion(f32[2048,1,5,128]{0,3,2,1:T(8,128)} %get-tuple-element.329, f32[1024,2048,5]{1,0,2:T(8,128)} %get-tuple-element.310, f32[2048,5]{0,1:T(8,128)S(1)} %get-tuple-element.308, pred[1024]{0:T(1024)(128)(4,1)S(1)} %add_compare_fusion.2, f32[2048,5]{0,1:T(8,128)S(1)} %get-tuple-element.312, ...), kind=kOutput, calls=%fused_computation.11.clone.1 | convolution fusion | flops 2731540480 | bytes 52889604 | tf_op jit(solution)/shard_map/while/body/eval_jaxpr/rkgj,kjd->rkgd/dot_general | solution.py:80
  257.5 3.9 all-to-all-start.2
  261.7 1.7 fusion.67
  263.5 1.7 fusion.64
  265.8 25.6 %all-to-all-done.2 = bf16[32,2048,1,5]{1,3,2,0:T(8,128)(2,1)S(1)} async-done(((bf16[32,2048,1,5]{1,3,2,0:T(8,128)(2,1)}), bf16[32,2048,1,5]{1,3,2,0:T(8,128)(2,1)S(1)}, u32[]{:S(2)}, u32[]{:S(2)}) %all-to-all-start.2) | async-done | bytes 655392 | tf_op jit(solution)/shard_map/all_to_all | solution.py:24
  291.7 3.2 multiply_convert_fusion
  295.1 4.7 %copy.73 = bf16[2048,1,5,128]{3,2,0,1:T(8,128)(2,1)} copy(bf16[2048,1,5,128]{0,3,2,1:T(8,128)(2,1)S(1)} %multiply_convert_fusion) | data formatting | bytes 5242880 | tf_op jit(solution)/shard_map/convert_element_type | solution.py:178
  299.8 6.0 %convert_element_type.92 = bf16[16,2,64,640]{3,2,1,0:T(8,128)(2,1)S(1)} reshape(bf16[2048,1,5,128]{3,2,0,1:T(8,128)(2,1)} %copy.73) | data formatting | bytes 5242880 | tf_op jit(solution)/shard_map/convert_element_type | solution.py:178
  306.6 6.3 %all_to_all.41 = bf16[2,16,64,645]{3,2,1,0:T(8,128)(2,1)S(1)} all-to-all(bf16[2,16,64,645]{3,2,1,0:T(8,128)(2,1)S(1)} %copy.75), channel_id=1, replica_groups=mesh['blk_0'=8,'blk_1'=2,'blk_2'=2,'head'=8] {'blk_2'}, dimensions={0} | all-to-all | bytes 5283840 | tf_op jit(solution)/shard_map/all_to_all | solution.py:51
  312.9 2.3 reduce_sum.67
  315.2 4.4 %all-to-all-start.4 = ((bf16[16,64,645]{2,1,0:T(8,128)(2,1)}), bf16[16,64,645]{2,1,0:T(8,128)(2,1)}, u32[]{:S(2)}, u32[]{:S(2)}) async-start(bf16[16,64,645]{2,1,0:T(8,128)(2,1)} %reduce_sum.67), calls=%async_computation.4 | async-start | bytes 3145728 | tf_op jit(solution)/shard_map/all_to_all | solution.py:59
  319.7 15.8 %all-gather.5.cloned.1.call-done = bf16[2048,256]{1,0:T(8,128)(2,1)} async-done(((bf16[64,256]{1,0:T(8,128)(2,1)}), bf16[2048,256]{1,0:T(8,128)(2,1)}) %all-gather.5.cloned.1.call-update) | async-done | bytes 1048592 | tf_op jit(solution)/shard_map/all_gather | solution.py:18
  335.6 1.7 fusion.85
  338.3 21.6 %all-to-all-done.4 = bf16[16,64,645]{2,1,0:T(8,128)(2,1)} async-done(((bf16[16,64,645]{2,1,0:T(8,128)(2,1)}), bf16[16,64,645]{2,1,0:T(8,128)(2,1)}, u32[]{:S(2)}, u32[]{:S(2)}) %all-to-all-start.4) | async-done | bytes 1320992 | tf_op jit(solution)/shard_map/all_to_all | solution.py:59
  362.5 1.7 fusion.58
  364.5 38.0 %all_to_all.42 = bf16[16,64,640]{2,1,0:T(8,128)(2,1)S(1)} all-to-all(bf16[16,64,640]{2,1,0:T(8,128)(2,1)S(1)} %broadcast_in_dim.130), channel_id=1, replica_groups=mesh['blk_0'=8,'blk_1'=2,'blk_2'=2,'head'=8] {'blk_0','blk_1'}, dimensions={0} | all-to-all | bytes 2621440 | tf_op jit(solution)/shard_map/all_to_all | solution.py:24
  402.9 5.8 %all_to_all.43 = bf16[2,16,64,640]{3,2,1,0:T(8,128)(2,1)S(1)} all-to-all(bf16[2,16,64,640]{3,2,1,0:T(8,128)(2,1)S(1)} %broadcast_in_dim.131), channel_id=1, replica_groups=mesh['blk_0'=8,'blk_1'=2,'blk_2'=2,'head'=8] {'blk_2'}, dimensions={0} | all-to-all | bytes 5242880 | tf_op jit(solution)/shard_map/all_to_all | solution.py:24
  410.1 18.8 %all_to_all.44 = bf16[8,256,160]{1,2,0:T(8,128)(2,1)S(1)} all-to-all(bf16[8,256,160]{1,2,0:T(8,128)(2,1)S(1)} %bitcast.236), channel_id=1, replica_groups=mesh['blk_0'=8,'blk_1'=2,'blk_2'=2,'head'=8] {'head'}, dimensions={0} | all-to-all | bytes 1310720 | tf_op jit(solution)/shard_map/all_to_all | solution.py:51
  (77 shorter events, 15.1 us)
Async XLA Ops:
  6.5 402.5 %copy-start = (bf16[640,160]{0,1:T(8,128)(2,1)S(1)}, bf16[640,160]{0,1:T(8,128)(2,1)}, u32[]{:S(2)}) copy-start(bf16[640,160]{0,1:T(8,128)(2,1)} %param.17) | copy-start | bytes 614404
  6.5 78.9 %all-gather.3.cloned.1.call-start = ((), (), s32[]{:S(2)}) async-start(), calls=%async_computation.8 | async-start | bytes 9461760 | tf_op jit(solution)/shard_map/all_gather | solution.py:18
  9.0 80.8 %copy-start.5 = (f32[64]{0:T(128)}, f32[64]{0:T(128)S(1)}, u32[]{:S(2)}) copy-start(f32[64]{0:T(128)S(1)} %add_multiply_fusion) | copy-start | bytes 772
  10.3 79.5 %copy-start.9 = (f32[64]{0:T(128)}, f32[64]{0:T(128)S(1)}, u32[]{:S(2)}) copy-start(f32[64]{0:T(128)S(1)} %add_rsqrt_fusion) | copy-start | bytes 772
  89.8 0.6 copy-start.3
  91.7 40.2 %all-to-all-start = ((bf16[16,64,640]{2,1,0:T(8,128)(2,1)}), bf16[16,64,640]{2,1,0:T(8,128)(2,1)S(1)}, u32[]{:S(2)}, u32[]{:S(2)}) async-start(bf16[16,64,640]{2,1,0:T(8,128)(2,1)} %broadcast_in_dim.122), calls=%async_computation | async-start | bytes 2621440 | tf_op jit(solution)/shard_map/all_to_all | solution.py:24
  142.6 2.6 copy-start.1
  162.2 18.5 %copy-start.7 = (bf16[1,2048,128]{2,1,0:T(8,128)(2,1)S(1)}, bf16[1,2048,128]{2,1,0:T(8,128)(2,1)}, u32[]{:S(2)}) copy-start(bf16[1,2048,128]{2,1,0:T(8,128)(2,1)} %get-tuple-element.345) | copy-start | bytes 1572868 | tf_op jit(solution)/shard_map/while
  216.9 18.5 %copy-start.7 = (bf16[1,2048,128]{2,1,0:T(8,128)(2,1)S(1)}, bf16[1,2048,128]{2,1,0:T(8,128)(2,1)}, u32[]{:S(2)}) copy-start(bf16[1,2048,128]{2,1,0:T(8,128)(2,1)} %get-tuple-element.345) | copy-start | bytes 1572868 | tf_op jit(solution)/shard_map/while
  256.4 5.3 %copy-start.2 = (bf16[64,5120]{1,0:T(8,128)(2,1)S(1)}, bf16[64,5120]{1,0:T(8,128)(2,1)}, u32[]{:S(2)}) copy-start(bf16[64,5120]{1,0:T(8,128)(2,1)} %param.12) | copy-start | bytes 1966084
  256.4 5.3 %copy-start.8 = (f32[5120]{0:T(1024)S(1)}, f32[5120]{0:T(1024)}, u32[]{:S(2)}) copy-start(f32[5120]{0:T(1024)} %param.13) | copy-start | bytes 61444
  256.4 5.3 %copy-start.10 = (f32[64]{0:T(128)S(1)}, f32[64]{0:T(128)}, u32[]{:S(2)}) copy-start(f32[64]{0:T(128)} %copy-done.9) | copy-start | bytes 772
  257.5 33.9 %all-to-all-start.2 = ((bf16[32,2048,1,5]{1,3,2,0:T(8,128)(2,1)}), bf16[32,2048,1,5]{1,3,2,0:T(8,128)(2,1)S(1)}, u32[]{:S(2)}, u32[]{:S(2)}) async-start(bf16[32,2048,1,5]{1,3,2,0:T(8,128)(2,1)} %broadcast_in_dim.125), calls=%async_computation.2 | async-start | bytes 2097152 | tf_op jit(solution)/shard_map/all_to_all | solution.py:24
  261.5 74.1 %all-gather.5.cloned.1.call-start = ((), (), s32[]{:S(2)}) async-start(), calls=%async_computation.9 | async-start | bytes 1081344 | tf_op jit(solution)/shard_map/all_gather | solution.py:18
  312.9 22.7 %copy-start.4 = (bf16[64,640]{1,0:T(8,128)(2,1)S(1)}, bf16[64,640]{1,0:T(8,128)(2,1)}, u32[]{:S(2)}) copy-start(bf16[64,640]{1,0:T(8,128)(2,1)} %copy-done.3) | copy-start | bytes 245764
  312.9 22.7 %copy-start.6 = (f32[64]{0:T(128)S(1)}, f32[64]{0:T(128)}, u32[]{:S(2)}) copy-start(f32[64]{0:T(128)} %copy-done.5) | copy-start | bytes 772
  315.2 44.7 %all-to-all-start.4 = ((bf16[16,64,645]{2,1,0:T(8,128)(2,1)}), bf16[16,64,645]{2,1,0:T(8,128)(2,1)}, u32[]{:S(2)}, u32[]{:S(2)}) async-start(bf16[16,64,645]{2,1,0:T(8,128)(2,1)} %reduce_sum.67), calls=%async_computation.4 | async-start | bytes 3145728 | tf_op jit(solution)/shard_map/all_to_all | solution.py:59
Sparse Core Ops, SparseCore 0:
  9.2 76.1 all-gather.2
  265.9 69.5 all-gather.4
where the time goes:
time: 439 us; the launch traced here: 436 us
  waiting for transfers between devices  173 us (39%)
  matrix products  85 us (19%)
  blocking collectives  74.8 us (17%)
  other arithmetic  51.4 us (12%)
  local copies, waits for them, and re-layouts  23.9 us (5%)
  between operations  14.4 us (3%)
  starting transfers between devices  14.1 us (3%)
    all_gather x2, waiting for transfers between devices, sent_together(): whole = lax.all_gather(both, axis, axis=dim, tiled=True)  90.9 us
    all_to_all x2, waiting for transfers between devices, copy_for_each(): lax.all_to_all(jnp.broadcast_to(x[None], (size, *x.shape)), axis, 0, 0, t...  60.3 us
    all_to_all x3, blocking collectives, copy_for_each(): lax.all_to_all(jnp.broadcast_to(x[None], (size, *x.shape)), axis, 0, 0, t...  49.7 us
    dot_general x3, matrix products, block_stats(): jnp.einsum('rkgj,kjd->rkgd', weights.astype(jnp.bfloat16), value_block, p...  42.1 us
    reduce_sum x3, other arithmetic, block_stats(): denominator = jnp.sum(weights, axis=-1)  37.5 us
    dot_general x3, matrix products, block_stats(): jnp.einsum('rkgd,kjd->rkgj', queries, key_block, preferred_element_type=j...  34.1 us
    all_to_all x2, blocking collectives, summed_on_arrival(): parts = lax.all_to_all(split_up(x, dim, size), axis, 0, 0, tiled=True)  25.1 us
    all_to_all x1, waiting for transfers between devices, sum_by_axis(): lax.all_to_all(nearer.astype(jnp.bfloat16), far, split_axis=0, concat_axi...  21.6 us
  transfers between devices with their start and end apart: 5, of which 5 were waited for; matrix products, arithmetic and copies ran while one was open for 6% of the time, Pallas kernels for 0%

commit v1 on v0

v1 whole, which is shorter than its diff:
```python
import functools

import jax
import jax.numpy as jnp
from jax import lax
from jax.experimental import pallas as pl
from jax.experimental.pallas import tpu as pltpu
from jax.sharding import Mesh
from jax.sharding import PartitionSpec as P

BLK = ("z", "y", "c")
BF = jnp.bfloat16
F32 = jnp.float32
NEG = -1e30
KEYS = 512


def shift(x, axis, d):
    n = lax.axis_size(axis)
    return lax.ppermute(x, axis, [(i, (i + d) % n) for i in range(n)])


def ring(x, axis):
    n = lax.axis_size(axis)
    ahead, behind = [x], [x]
    for step in range(n // 2):
        ahead.append(shift(ahead[-1], axis, 1))
        if step < (n - 1) // 2:
            behind.append(shift(behind[-1], axis, -1))
    return ahead + behind[:0:-1]


def nt(a, b):
    return lax.dot_general(a, b, (((1,), (1,)), ((), ())), preferred_element_type=F32)


def tn(a, b):
    return lax.dot_general(a, b, (((0,), (0,)), ((), ())), preferred_element_type=F32)


VM = pl.BlockSpec(memory_space=pltpu.VMEM)
SM = pl.BlockSpec(memory_space=pltpu.SMEM)


def params(mib=56):
    return pltpu.CompilerParams(vmem_limit_bytes=mib << 20)


def project(where, x, blocks):
    rows, _ = x.shape
    n = len(blocks)
    r, cols = blocks[0].shape
    t = rows // 4

    def kernel(where_ref, x_ref, *refs):
        w_refs, (keep, send, whole, total) = refs[:n], refs[n:]
        z, c = where_ref[0], where_ref[2]
        for d in range(n):
            at = lax.rem(z + (n - d), n)
            whole[pl.ds(pl.multiple_of(at * r, 16), r), :] = w_refs[d][...]
        total[...] = jnp.dot(x_ref[...], whole[...], preferred_element_type=F32).reshape(4, t, cols)
        for y in range(2):
            keep[y] = total[2 * y + c]
            send[y] = total[2 * y + 1 - c]

    half = jax.ShapeDtypeStruct((2, t, cols), F32)
    return pl.pallas_call(
        kernel,
        out_shape=[half, half],
        in_specs=[SM, VM] + [VM] * n,
        out_specs=[VM, VM],
        scratch_shapes=[pltpu.VMEM((n * r, cols), BF), pltpu.VMEM((4, t, cols), F32)],
        compiler_params=params(),
        name="project",
    )(where, x, *blocks)


def pack_cache(lens, keys, values):
    n = len(keys)
    rows, d = keys[0].shape
    room = n * rows + 4 * KEYS

    def kernel(len_ref, *refs):
        k_in, v_in, (k_out, v_out) = refs[:n], refs[n : 2 * n], refs[2 * n :]
        first = k_in[0][0:1, :]
        at = jnp.int32(0)
        for i in range(n):
            length = len_ref[i]
            at = pl.multiple_of(at, 16)
            k_out[pl.ds(at, rows), :] = k_in[i][...]
            v_out[pl.ds(at, rows), :] = v_in[i][...]
            whole = length // 16
            odd = length - whole * 16
            tail = pl.multiple_of(at + whole * 16, 16)

            @pl.when(odd > 0)
            def _():
                counted = lax.broadcasted_iota(jnp.int32, (16, d), 0) < odd
                k_tile = k_out[pl.ds(tail, 16), :].astype(F32)
                v_tile = v_out[pl.ds(tail, 16), :].astype(F32)
                k_out[pl.ds(tail, 16), :] = jnp.where(counted, k_tile, first.astype(F32)).astype(BF)
                v_out[pl.ds(tail, 16), :] = jnp.where(counted, v_tile, 0.0).astype(BF)

            at = at + ((length + 15) // 16) * 16
        at = pl.multiple_of(at, 16)
        k_out[pl.ds(at, 2 * KEYS), :] = jnp.broadcast_to(first, (2 * KEYS, d))
        v_out[pl.ds(at, 2 * KEYS), :] = jnp.zeros((2 * KEYS, d), BF)

    out = jax.ShapeDtypeStruct((room, d), BF)
    return pl.pallas_call(
        kernel,
        out_shape=[out, out],
        in_specs=[SM] + [VM] * (2 * n),
        out_specs=[VM, VM],
        compiler_params=params(),
        name="pack_cache",
    )(lens, *keys, *values)


def attend(lens, where, chunks, dists, k_all, v_all, new_pairs):
    n = len(chunks)
    t, width = chunks[0].shape
    d = k_all.shape[1]
    g = width // d
    rows = n * g * t
    shards = lens.shape[0]
    fresh = new_pairs[0][0].shape[0]

    def kernel(len_ref, where_ref, *refs):
        q_refs = refs[:n]
        k_ref, v_ref, nk0, nv0, nk1, nv1 = refs[n : n + 6]
        outs = refs[n + 6 : 2 * n + 6]
        q_all, m, l, acc, s_a, s_b, token, stats = refs[2 * n + 6 :]
        z, y, c = where_ref[0], where_ref[1], where_ref[2]
        nz = where_ref[3]
        for i in range(n):
            base = lax.rem(z + nz - dists[i], nz) * (4 * t) + (2 * y + c) * t
            for h in range(g):
                at = (i * g + h) * t
                q_all[at : at + t, :] = q_refs[i][:, h * d : (h + 1) * d]
            span = slice(i * g * t, (i + 1) * g * t)
            token[:, span] = base + lax.rem(lax.broadcasted_iota(jnp.int32, (1, g * t), 1), t)
        m[...] = jnp.full(m.shape, NEG, F32)
        l[...] = jnp.zeros(l.shape, F32)
        acc[...] = jnp.zeros(acc.shape, F32)

        def scores(at):
            return nt(k_ref[pl.ds(pl.multiple_of(at, KEYS), KEYS), :], q_all[...])

        def absorb(s, values):
            before = m[...]
            now = jnp.maximum(before, jnp.max(s, axis=0, keepdims=True))
            fade = jnp.exp(before - now)
            p = jnp.exp(s - now)
            l[...] = l[...] * fade + jnp.sum(p, axis=0, keepdims=True)
            m[...] = now
            acc[...] = acc[...] * fade + tn(values, p.astype(BF))

        def values_at(at):
            return v_ref[pl.ds(pl.multiple_of(at, KEYS), KEYS), :]

        counted = jnp.int32(0)
        used = jnp.int32(0)
        for i in range(shards):
            counted = counted + len_ref[i]
            used = used + ((len_ref[i] + 15) // 16) * 16
        pairs = (used + 2 * KEYS - 1) // (2 * KEYS)
        s_a[...] = scores(0)

        def visit(u, _):
            at = u * (2 * KEYS)
            s_b[...] = scores(at + KEYS)
            absorb(s_a[...], values_at(at))
            s_a[...] = scores(at + 2 * KEYS)
            absorb(s_b[...], values_at(at + KEYS))
            return 0

        lax.fori_loop(0, pairs, visit, 0)
        extra = (pairs * (2 * KEYS) - counted).astype(F32)
        first = nt(k_ref[0:8, :], q_all[...])[0:1]
        l[...] = l[...] - extra * jnp.exp(first - m[...])
        for part, (nk, nv) in enumerate(((nk0, nv0), (nk1, nv1))):
            row = lax.broadcasted_iota(jnp.int32, (fresh, 1), 0)
            side = c if part == 0 else 1 - c
            key_token = z * (4 * t) + (row // t) * (2 * t) + side * t + lax.rem(row, t)
            s = nt(nk[...], q_all[...])
            s = jnp.where(key_token <= token[...], s, NEG)
            absorb(s, nv[...])
        top = m[...]
        top_hi = top.astype(BF).astype(F32)
        top_lo = (top - top_hi).astype(BF).astype(F32)
        scale = jnp.exp(top - (top_hi + top_lo))
        den = l[...] * scale
        den_hi = den.astype(BF).astype(F32)
        den_lo = den - den_hi
        numer = (acc[...] * scale).T
        stats[...] = jnp.zeros(stats.shape, F32)
        for i in range(n):
            for h in range(g):
                at = slice((i * g + h) * t, (i * g + h + 1) * t)
                outs[i][:, h * d : (h + 1) * d] = numer[at].astype(BF)
                for k, row in enumerate((top_hi, top_lo, den_hi, den_lo)):
                    stats[8 * k + h : 8 * k + h + 1, :] = row[:, at]
            outs[i][:, g * d :] = stats[...].T.astype(BF)

    out = jax.ShapeDtypeStruct((t, width + 128), BF)
    return pl.pallas_call(
        kernel,
        out_shape=[out] * n,
        in_specs=[SM, SM] + [VM] * (n + 6),
        out_specs=[VM] * n,
        scratch_shapes=[
            pltpu.VMEM((rows, d), BF),
            pltpu.VMEM((1, rows), F32),
            pltpu.VMEM((1, rows), F32),
            pltpu.VMEM((d, rows), F32),
            pltpu.VMEM((KEYS, rows), F32),
            pltpu.VMEM((KEYS, rows), F32),
            pltpu.VMEM((1, rows), jnp.int32),
            pltpu.VMEM((128, t), F32),
        ],
        compiler_params=params(),
        name="attend",
    )(lens, where, *chunks, k_all, v_all, *new_pairs[0], *new_pairs[1])


def merge(parts, d):
    n = len(parts)
    t, width = parts[0].shape
    g = (width - 128) // d

    def kernel(*refs):
        ins, out = refs[:n], refs[n]
        stats = [r[:, g * d :].astype(F32) for r in ins]
        for h in range(g):
            tops = [s[:, h : h + 1] + s[:, 8 + h : 9 + h] for s in stats]
            dens = [s[:, 16 + h : 17 + h] + s[:, 24 + h : 25 + h] for s in stats]
            top = functools.reduce(jnp.maximum, tops)
            shares = [jnp.exp(a - top) for a in tops]
            den = sum(w * a for w, a in zip(shares, dens))
            num = sum(w * r[:, h * d : (h + 1) * d].astype(F32) for w, r in zip(shares, ins))
            out[:, h * d : (h + 1) * d] = (num / den).astype(BF)

    return pl.pallas_call(
        kernel,
        out_shape=jax.ShapeDtypeStruct((t, g * d), BF),
        in_specs=[VM] * n,
        out_specs=VM,
        compiler_params=params(),
        name="merge",
    )(*parts)


def per_device(
    hidden,
    norm_gain,
    w_query,
    key_projection_weight,
    value_projection_weight,
    w_out,
    cache_keys,
    earlier_values,
    cache_len,
    stretch_start,
):
    t, model = hidden.shape
    d = cache_keys.shape[2]
    q_cols = w_query.shape[1]
    kv_cols = key_projection_weight.shape[1]
    nz = lax.axis_size("z")
    nh = lax.axis_size("head")
    z, y, c = lax.axis_index("z"), lax.axis_index("y"), lax.axis_index("c")
    where = jnp.stack([z, y, c, jnp.int32(nz)]).astype(jnp.int32)

    weights = jnp.concatenate([w_query, key_projection_weight, value_projection_weight], axis=1)
    blocks = ring(weights, "z")

    stream = hidden.astype(F32)
    normed = (
        stream * lax.rsqrt(jnp.mean(stream * stream, axis=-1, keepdims=True) + 1e-05) * norm_gain
    ).astype(BF)
    cut = normed.reshape(t, nz, 4, model // (4 * nz)).transpose(2, 0, 1, 3).reshape(4, t, model // 4)
    x = lax.all_to_all(cut, ("y", "c"), 0, 0, tiled=True).reshape(4 * t, model // 4)

    near = (cache_keys[0], earlier_values[0], cache_len)
    beside = tuple(shift(a, "y", 1) for a in near)
    four = [near, beside] + [tuple(shift(a, "c", 1) for a in s) for s in (near, beside)]
    lens = jnp.concatenate([s[2] for s in four])
    k_all, v_all = pack_cache(lens, [s[0] for s in four], [s[1] for s in four])

    out_beside = shift(w_out, "y", 1)
    out_four = [w_out, shift(w_out, "c", 1), out_beside, shift(out_beside, "c", 1)]

    keep, send = project(where, x, blocks)
    both = keep + shift(send, "c", 1)
    q_near = lax.dynamic_index_in_dim(both, y, 0, keepdims=False)[:, :q_cols]
    q_away = lax.dynamic_index_in_dim(both, 1 - y, 0, keepdims=False)[:, :q_cols]
    kv = both[:, :, q_cols:]
    queries = (q_near + shift(q_away, "y", 1)).astype(BF)
    fresh = (kv + shift(kv, "y", 1)).astype(BF).reshape(2 * t, 2 * kv_cols)
    other = shift(fresh, "c", 1)
    new_pairs = [(f[:, :kv_cols], f[:, kv_cols:]) for f in (fresh, other)]

    token = lax.axis_index(BLK) * t + jnp.arange(t, dtype=jnp.int32)
    positions = stretch_start[0] + token
    temper = jnp.log(((positions + 1) // 8192).astype(F32) + 1.0) * 0.1 + 1.0
    scaled = (
        lax.optimization_barrier(queries).astype(F32) * (temper * d ** (-0.5))[:, None]
    ).astype(BF)

    chunks = ring(scaled, "z")
    partial = attend(lens, where, chunks, list(range(nz)), k_all, v_all, new_pairs)
    order = lax.rem(z - jnp.arange(nz) + nz, nz)
    stacked = jnp.stack(partial)[order]
    returned = lax.all_to_all(stacked, "z", 0, 0, tiled=True)
    context = merge([returned[i] for i in range(nz)], d)

    spread = lax.all_gather(context, "z", axis=0, tiled=False)
    tokens = spread.reshape(nz * t, q_cols)
    terms = [jnp.dot(tokens, w, preferred_element_type=F32).astype(BF) for w in out_four]
    terms = jnp.stack(terms, 1).reshape(nz, t, 4, -1).transpose(0, 2, 1, 3)
    summed = lax.all_to_all(terms, "head", 0, 0, tiled=True).astype(F32).sum(axis=0).astype(BF)
    here = 2 * y + c
    summed = summed[jnp.arange(4) ^ here]
    final = lax.all_to_all(summed, ("y", "c"), 0, 0, tiled=True)
    return final.reshape(4 * t, -1)


def solution(mesh):
    finer = Mesh(mesh.devices.reshape(8, 2, 2, mesh.shape["head"]), ("z", "y", "c", "head"))
    return jax.shard_map(
        per_device,
        mesh=finer,
        in_specs=(
            P(BLK, None),
            P(),
            P(BLK, "head"),
            P(BLK, "head"),
            P(BLK, "head"),
            P("head", BLK),
            P("head", BLK, None),
            P("head", BLK, None),
            P(BLK),
            P(),
        ),
        out_specs=P("head", BLK),
        check_vma=False,
    )
```

time: 439 us -> 243 us (0.55)
  waiting for transfers between devices: 173 us -> 84.7 us
  matrix products: 85 us -> 1.47 us
  other arithmetic: 51.4 us -> 7.3 us
  blocking collectives: 74.8 us -> 33 us
  Pallas kernels: 0 us -> 41.1 us
  starting transfers between devices: 14.1 us -> 47.6 us
  between operations: 14.4 us -> 1.79 us
    all_gather x2 -> x0, waiting for transfers between devices: 90.9 us -> none  [sent_together(): whole = lax.all_gather(both, axis, axis=dim, tiled=True)]
    dot_general x10 -> x4, matrix products: 85 us -> 1.47 us  [per_device(): jnp.dot(tokens, w, preferred_element_type=F32).astype(BF)]
    all_to_all x5 -> x1, blocking collectives: 74.8 us -> 7.02 us  [per_device(): final = lax.all_to_all(summed, ('y', 'c'), 0, 0, tiled=True)]
    ppermute x0 -> x30, waiting for transfers between devices: none -> 53 us  [shift(): return lax.ppermute(x, axis, [(i, (i + d) % n) for i in range(n)])]
    all_to_all x3, waiting for transfers between devices: 81.8 us -> 31.7 us  [the longest x1 13.7 us: per_device(): returned = lax.all_to_all(stacked, 'z', 0, 0, tiled=True)]
    reduce_sum x6 -> x1, other arithmetic: 42.1 us -> 0.18 us  [per_device(): lax.all_to_all(terms, 'head', 0, 0, tiled=True).astype(F32).sum(axis=0)]
    pallas_call x0 -> x4, Pallas kernels: none -> 41.1 us  [the longest x1 29.9 us: attend(): pl.pallas_call(kernel, out_shape=[out] * n, in_specs=[SM, SM] + [VM] * (n...]
    ppermute x0 -> x30, starting transfers between devices: none -> 30.2 us  [shift(): return lax.ppermute(x, axis, [(i, (i + d) % n) for i in range(n)])]
  transfers between devices with their start and end apart: 5 -> 33, of which waited for: 5 -> 16; matrix products, arithmetic and copies ran while one was open for 6% -> 6% of each run, Pallas kernels for 0% -> 3%
where the time goes in v1:
time: 243 us; the launch traced here: 241 us
  waiting for transfers between devices  84.7 us (35%)
  starting transfers between devices  47.6 us (20%)
  Pallas kernels  41.1 us (17%)
  blocking collectives  33 us (14%)
  local copies, waits for them, and re-layouts  23.7 us (10%)
  other arithmetic  7.3 us (3%)
    ppermute x30, waiting for transfers between devices, shift(): return lax.ppermute(x, axis, [(i, (i + d) % n) for i in range(n)])  53 us
    ppermute x30, starting transfers between devices, shift(): return lax.ppermute(x, axis, [(i, (i + d) % n) for i in range(n)])  30.2 us
    pallas_call x1, Pallas kernels, attend(): pl.pallas_call(kernel, out_shape=[out] * n, in_specs=[SM, SM] + [VM] * (n...  29.9 us
    all_gather x1, blocking collectives, per_device(): spread = lax.all_gather(context, 'z', axis=0, tiled=False)  25.9 us
    all_to_all x1, waiting for transfers between devices, per_device(): returned = lax.all_to_all(stacked, 'z', 0, 0, tiled=True)  13.7 us
    all_to_all x1, waiting for transfers between devices, per_device(): lax.all_to_all(terms, 'head', 0, 0, tiled=True).astype(F32).sum(axis=0)  11.8 us
    unnamed x63, local copies, waits for them, and re-layouts  11.4 us
    all_to_all x1, starting transfers between devices, per_device(): lax.all_to_all(terms, 'head', 0, 0, tiled=True).astype(F32).sum(axis=0)  7.46 us
  transfers between devices with their start and end apart: 33, of which 16 were waited for; matrix products, arithmetic and copies ran while one was open for 6% of the time, Pallas kernels for 3%

profile of v1, /device:TPU:2, one launch (start us, length us, event | category | flops | bytes accessed | tf_op | source)
XLA Modules:
  0.0 240.6 jit_solution(2896213431392920120)
XLA Ops:
  2.6 2.0 collective-permute-start.3
  4.6 4.0 %collective-permute-start.7 = (bf16[160,896]{1,0:T(8,128)(2,1)S(1)}, bf16[160,896]{1,0:T(8,128)(2,1)S(1)}, u32[]{:S(2)}, u32[]{:S(2)}) collective-permute-start(bf16[160,896]{1,0:T(8,128)(2,1)S(1)} %constant_dynamic-update-slice_fusion.refs_0_), channel_id=1, source_target_pairs={{0,224},{32,0},{64,32},{96,64},{128,96},{160,128},{192,160},{224,1... | collective-permute-start | bytes 860168 | tf_op jit(solution)/shard_map/ppermute | solution.py:20
  8.6 6.7 %collective-permute-done.3.refs_1_ = bf16[160,896]{1,0:T(8,128)(2,1)S(1)} collective-permute-done((bf16[160,896]{1,0:T(8,128)(2,1)S(1)}, bf16[160,896]{1,0:T(8,128)(2,1)S(1)}, u32[]{:S(2)}, u32[]{:S(2)}) %collective-permute-start.3) | collective-permute-done | bytes 286752 | tf_op jit(solution)/shard_map/ppermute | solution.py:20
  16.8 3.2 %collective-permute-start.8 = (bf16[160,896]{1,0:T(8,128)(2,1)S(1)}, bf16[160,896]{1,0:T(8,128)(2,1)S(1)}, u32[]{:S(2)}, u32[]{:S(2)}) collective-permute-start(bf16[160,896]{1,0:T(8,128)(2,1)S(1)} %collective-permute-done.7.refs_7_), channel_id=1, source_target_pairs={{0,224},{32,0},{64,32},{96,64},{128,96},{160,128},{192,160},{224,1... | collective-permute-start | bytes 860168 | tf_op jit(solution)/shard_map/ppermute | solution.py:20
  20.1 4.6 %collective-permute-done.4.refs_2_ = bf16[160,896]{1,0:T(8,128)(2,1)S(1)} collective-permute-done((bf16[160,896]{1,0:T(8,128)(2,1)S(1)}, bf16[160,896]{1,0:T(8,128)(2,1)S(1)}, u32[]{:S(2)}, u32[]{:S(2)}) %collective-permute-start.4) | collective-permute-done | bytes 286752 | tf_op jit(solution)/shard_map/ppermute | solution.py:20
  26.9 2.0 reshape.117
  29.0 3.5 %all-to-all-start = ((bf16[4,64,1280]{2,1,0:T(8,128)(2,1)}), bf16[4,64,1280]{2,1,0:T(8,128)(2,1)S(1)}, u32[]{:S(2)}, u32[]{:S(2)}) async-start(bf16[4,64,1280]{2,1,0:T(8,128)(2,1)} %reshape.117), calls=%async_computation | async-start | bytes 1310720 | tf_op jit(solution)/shard_map/all_to_all | solution.py:283
  32.5 3.3 %collective-permute-start.9 = (bf16[160,896]{1,0:T(8,128)(2,1)S(1)}, bf16[160,896]{1,0:T(8,128)(2,1)S(1)}, u32[]{:S(2)}, u32[]{:S(2)}) collective-permute-start(bf16[160,896]{1,0:T(8,128)(2,1)S(1)} %collective-permute-done.8.refs_6_), channel_id=1, source_target_pairs={{0,224},{32,0},{64,32},{96,64},{128,96},{160,128},{192,160},{224,1... | collective-permute-start | bytes 860168 | tf_op jit(solution)/shard_map/ppermute | solution.py:20
  36.4 6.2 %all-to-all-done = bf16[4,64,1280]{2,1,0:T(8,128)(2,1)S(1)} async-done(((bf16[4,64,1280]{2,1,0:T(8,128)(2,1)}), bf16[4,64,1280]{2,1,0:T(8,128)(2,1)S(1)}, u32[]{:S(2)}, u32[]{:S(2)}) %all-to-all-start) | async-done | bytes 655392 | tf_op jit(solution)/shard_map/all_to_all | solution.py:283
  42.7 3.3 %collective-permute-done.6.refs_4_ = bf16[160,896]{1,0:T(8,128)(2,1)S(1)} collective-permute-done((bf16[160,896]{1,0:T(8,128)(2,1)}, bf16[160,896]{1,0:T(8,128)(2,1)S(1)}, u32[]{:S(2)}, u32[]{:S(2)}) %collective-permute-start.6) | collective-permute-done | bytes 286752 | tf_op jit(solution)/shard_map/ppermute | solution.py:20
  46.7 3.8 %project.1 = (f32[2,64,896]{2,1,0:T(8,128)}, f32[2,64,896]{2,1,0:T(8,128)}) custom-call(s32[4]{0:T(128)} %pad_add_fusion.1.where_ref, bf16[256,1280]{1,0:T(8,128)(2,1)} %bitcast.72, bf16[160,896]{1,0:T(8,128)(2,1)} %copy-done.2, bf16[160,896]{1,0:T(8,128)(2,1)} %copy-done.12, bf16[160,896]{1,0:T(8,128)(2,1)} %copy-done.14, ...), custom_call_target="tpu_custom_call" | custom-call | tf_op jit(solution)/shard_map/project/pallas_call | solution.py:67
  50.6 1.8 collective-permute-start.19
  57.9 7.5 %collective-permute-done.19.refs_1_ = bf16[2048,128]{1,0:T(8,128)(2,1)S(1)} collective-permute-done((bf16[2048,128]{1,0:T(8,128)(2,1)S(1)}, bf16[2048,128]{1,0:T(8,128)(2,1)S(1)}, u32[]{:S(2)}, u32[]{:S(2)}) %collective-permute-start.19) | collective-permute-done | bytes 524320 | tf_op jit(solution)/shard_map/ppermute | solution.py:20
  65.4 11.2 %collective-permute-done.22.refs_5_ = bf16[2048,128]{1,0:T(8,128)(2,1)S(1)} collective-permute-done((bf16[2048,128]{1,0:T(8,128)(2,1)S(1)}, bf16[2048,128]{1,0:T(8,128)(2,1)S(1)}, u32[]{:S(2)}, u32[]{:S(2)}) %collective-permute-start.22) | collective-permute-done | bytes 524320 | tf_op jit(solution)/shard_map/ppermute | solution.py:20
  76.6 3.0 %collective-permute-done.11 = f32[64,640]{1,0:T(8,128)S(1)} collective-permute-done((f32[64,640]{1,0:T(8,128)}, f32[64,640]{1,0:T(8,128)S(1)}, u32[]{:S(2)}, u32[]{:S(2)}) %collective-permute-start.11) | collective-permute-done | bytes 163872 | tf_op jit(solution)/shard_map/ppermute | solution.py:20
  85.2 2.5 %pad_add_fusion.len_ref = s32[4]{0:T(128)} fusion(s32[1]{0:T(128)} %collective-permute-done.2, s32[1]{0:T(128)} %collective-permute-done.1, s32[1]{0:T(128)} %collective-permute-done, s32[1]{0:T(128)S(6)} %copy.29), kind=kLoop, calls=%fused_computation.50 | loop fusion | flops 12 | bytes 32 | tf_op jit(solution)/shard_map/concatenate | solution.py:288
  89.6 4.9 %pack_cache.1 = (bf16[10240,128]{1,0:T(8,128)(2,1)}, bf16[10240,128]{1,0:T(8,128)(2,1)}) custom-call(s32[4]{0:T(128)} %pad_add_fusion.len_ref, bf16[2048,128]{1,0:T(8,128)(2,1)} %bitcast.73, bf16[2048,128]{1,0:T(8,128)(2,1)} %copy-done.5, bf16[2048,128]{1,0:T(8,128)(2,1)} %copy-done.7, bf16[2048,128]{1,0:T(8,128)(2,1)} %copy-done.9, ...), custom_call_target="tpu_custom_call" | custom-call | tf_op jit(solution)/shard_map/pack_cache/pallas_call | solution.py:110
  94.5 3.2 %collective-permute-start.16 = (bf16[64,640]{1,0:T(8,128)(2,1)S(1)}, bf16[64,640]{1,0:T(8,128)(2,1)S(1)}, u32[]{:S(2)}, u32[]{:S(2)}) collective-permute-start(bf16[64,640]{1,0:T(8,128)(2,1)S(1)} %multiply_convert_fusion.refs_0_), channel_id=1, source_target_pairs={{0,224},{32,0},{64,32},{96,64},{128,96},{160,128},{192,160},{224,1... | collective-permute-start | bytes 245768 | tf_op jit(solution)/shard_map/ppermute | solution.py:20
  97.8 1.9 collective-permute-done.16.refs_7_
  99.7 3.6 %collective-permute-start.17 = (bf16[64,640]{1,0:T(8,128)(2,1)S(1)}, bf16[64,640]{1,0:T(8,128)(2,1)S(1)}, u32[]{:S(2)}, u32[]{:S(2)}) collective-permute-start(bf16[64,640]{1,0:T(8,128)(2,1)S(1)} %collective-permute-done.16.refs_7_), channel_id=1, source_target_pairs={{0,224},{32,0},{64,32},{96,64},{128,96},{160,128},{192,160},{224,1... | collective-permute-start | bytes 245768 | tf_op jit(solution)/shard_map/ppermute | solution.py:20
  105.4 3.6 %collective-permute-start.18 = (bf16[64,640]{1,0:T(8,128)(2,1)S(1)}, bf16[64,640]{1,0:T(8,128)(2,1)S(1)}, u32[]{:S(2)}, u32[]{:S(2)}) collective-permute-start(bf16[64,640]{1,0:T(8,128)(2,1)S(1)} %collective-permute-done.17.refs_6_), channel_id=1, source_target_pairs={{0,224},{32,0},{64,32},{96,64},{128,96},{160,128},{192,160},{224,1... | collective-permute-start | bytes 245768 | tf_op jit(solution)/shard_map/ppermute | solution.py:20
  111.1 3.6 %collective-permute-done.15.refs_4_ = bf16[64,640]{1,0:T(8,128)(2,1)S(1)} collective-permute-done((bf16[64,640]{1,0:T(8,128)(2,1)S(1)}, bf16[64,640]{1,0:T(8,128)(2,1)S(1)}, u32[]{:S(2)}, u32[]{:S(2)}) %collective-permute-start.15) | collective-permute-done | bytes 81952 | tf_op jit(solution)/shard_map/ppermute | solution.py:20
  115.3 29.9 %attend.1 = (bf16[64,768]{1,0:T(8,128)(2,1)}, bf16[64,768]{1,0:T(8,128)(2,1)}, bf16[64,768]{1,0:T(8,128)(2,1)}, bf16[64,768]{1,0:T(8,128)(2,1)}, bf16[64,768]{1,...) custom-call(s32[4]{0:T(128)} %pad_add_fusion.len_ref, ...), custom_call_target="tpu_custom_call" | custom-call | tf_op jit(solution)/shard_map/attend/pallas_call | solution.py:207
  153.1 6.5 %all-to-all-start.1 = ((bf16[8,64,768]{2,1,0:T(8,128)(2,1)}), bf16[8,64,768]{2,1,0:T(8,128)(2,1)S(1)}, u32[]{:S(2)}, u32[]{:S(2)}) async-start(bf16[8,64,768]{2,1,0:T(8,128)(2,1)} %gather_fusion), calls=%async_computation.1 | async-start | bytes 1572864 | tf_op jit(solution)/shard_map/all_to_all | solution.py:315
  160.0 5.4 %collective-permute-done.28 = bf16[640,160]{0,1:T(8,128)(2,1)S(1)} collective-permute-done((bf16[640,160]{0,1:T(8,128)(2,1)S(1)}, bf16[640,160]{0,1:T(8,128)(2,1)S(1)}, u32[]{:S(2)}, u32[]{:S(2)}) %collective-permute-start.28) | collective-permute-done | bytes 204832 | tf_op jit(solution)/shard_map/ppermute | solution.py:20
  165.4 13.7 %all-to-all-done.1 = bf16[8,64,768]{2,1,0:T(8,128)(2,1)S(1)} async-done(((bf16[8,64,768]{2,1,0:T(8,128)(2,1)}), bf16[8,64,768]{2,1,0:T(8,128)(2,1)S(1)}, u32[]{:S(2)}, u32[]{:S(2)}) %all-to-all-start.1) | async-done | bytes 786464 | tf_op jit(solution)/shard_map/all_to_all | solution.py:315
  179.9 2.5 %merge.1 = bf16[64,640]{1,0:T(8,128)(2,1)} custom-call(bf16[64,768]{1,0:T(8,128)(2,1)} %get-tuple-element.36.refs_0_, bf16[64,768]{1,0:T(8,128)(2,1)} %get-tuple-element.35.refs_1_, bf16[64,768]{1,0:T(8,128)(2,1)} %get-tuple-element.34.refs_2_, bf16[64,768]{1,0:T(8,128)(2,1)} %get-tuple-element.33.refs_3_, bf16[64,768]{1,0:T(8,128)(2,1)} %get-tuple-element.32.refs_4_, ...), custom_call_target="tpu_custom_call" | custom-call | tf_op jit(solution)/shard_map/merge/pallas_call | solution.py:244
  182.4 25.9 %all-gather = bf16[512,640]{1,0:T(8,128)(2,1)S(1)} all-gather(bf16[64,640]{1,0:T(8,128)(2,1)} %merge.1), channel_id=2, replica_groups=mesh['z'=8,'y'=2,'c'=2,'head'=8] {'z'}, dimensions={0}, use_global_device_ids=true | all-gather | bytes 737280 | tf_op jit(solution)/shard_map/all_gather | solution.py:318
  211.0 1.8 copy.15
  212.8 7.5 %all-to-all-start.2 = ((bf16[8,4,64,160]{3,2,1,0:T(8,128)(2,1)}), bf16[8,4,64,160]{3,2,1,0:T(8,128)(2,1)S(1)}, u32[]{:S(2)}, u32[]{:S(2)}) async-start(bf16[8,4,64,160]{3,2,1,0:T(8,128)(2,1)} %copy.15), calls=%async_computation.2 | async-start | bytes 2097152 | tf_op jit(solution)/shard_map/all_to_all | solution.py:322
  220.2 11.8 %all-to-all-done.2 = bf16[8,4,64,160]{3,2,1,0:T(8,128)(2,1)S(1)} async-done(((bf16[8,4,64,160]{3,2,1,0:T(8,128)(2,1)}), bf16[8,4,64,160]{3,2,1,0:T(8,128)(2,1)S(1)}, u32[]{:S(2)}, u32[]{:S(2)}) %all-to-all-start.2) | async-done | bytes 655392 | tf_op jit(solution)/shard_map/all_to_all | solution.py:322
  232.8 7.0 %all_to_all.20 = bf16[4,64,160]{2,1,0:T(8,128)(2,1)S(1)} all-to-all(bf16[4,64,160]{2,1,0:T(8,128)(2,1)S(1)} %gather_fusion.1), channel_id=1, replica_groups=mesh['z'=8,'y'=2,'c'=2,'head'=8] {'y','c'}, dimensions={0} | all-to-all | bytes 163840 | tf_op jit(solution)/shard_map/all_to_all | solution.py:325
  (142 shorter events, 37.3 us)
Async XLA Ops:
  2.6 12.8 %collective-permute-start.3 = (bf16[160,896]{1,0:T(8,128)(2,1)S(1)}, bf16[160,896]{1,0:T(8,128)(2,1)S(1)}, u32[]{:S(2)}, u32[]{:S(2)}) collective-permute-start(bf16[160,896]{1,0:T(8,128)(2,1)S(1)} %constant_dynamic-update-slice_fusion.refs_0_), channel_id=1, source_target_pairs={{0,32},{32,64},{64,96},{96,128},{128,160},{160,192},{192,224},{224... | collective-permute-start | bytes 860168 | tf_op jit(solution)/shard_map/ppermute | solution.py:20
  4.6 12.2 %collective-permute-start.7 = (bf16[160,896]{1,0:T(8,128)(2,1)S(1)}, bf16[160,896]{1,0:T(8,128)(2,1)S(1)}, u32[]{:S(2)}, u32[]{:S(2)}) collective-permute-start(bf16[160,896]{1,0:T(8,128)(2,1)S(1)} %constant_dynamic-update-slice_fusion.refs_0_), channel_id=1, source_target_pairs={{0,224},{32,0},{64,32},{96,64},{128,96},{160,128},{192,160},{224,1... | collective-permute-start | bytes 860168 | tf_op jit(solution)/shard_map/ppermute | solution.py:20
  15.4 9.2 %collective-permute-start.4 = (bf16[160,896]{1,0:T(8,128)(2,1)S(1)}, bf16[160,896]{1,0:T(8,128)(2,1)S(1)}, u32[]{:S(2)}, u32[]{:S(2)}) collective-permute-start(bf16[160,896]{1,0:T(8,128)(2,1)S(1)} %collective-permute-done.3.refs_1_), channel_id=1, source_target_pairs={{0,32},{32,64},{64,96},{96,128},{128,160},{160,192},{192,224},{224... | collective-permute-start | bytes 860168 | tf_op jit(solution)/shard_map/ppermute | solution.py:20
  16.8 15.6 %collective-permute-start.8 = (bf16[160,896]{1,0:T(8,128)(2,1)S(1)}, bf16[160,896]{1,0:T(8,128)(2,1)S(1)}, u32[]{:S(2)}, u32[]{:S(2)}) collective-permute-start(bf16[160,896]{1,0:T(8,128)(2,1)S(1)} %collective-permute-done.7.refs_7_), channel_id=1, source_target_pairs={{0,224},{32,0},{64,32},{96,64},{128,96},{160,128},{192,160},{224,1... | collective-permute-start | bytes 860168 | tf_op jit(solution)/shard_map/ppermute | solution.py:20
  24.6 11.1 %collective-permute-start.5 = (bf16[160,896]{1,0:T(8,128)(2,1)S(1)}, bf16[160,896]{1,0:T(8,128)(2,1)}, u32[]{:S(2)}, u32[]{:S(2)}) collective-permute-start(bf16[160,896]{1,0:T(8,128)(2,1)S(1)} %collective-permute-done.4.refs_2_), channel_id=1, source_target_pairs={{0,32},{32,64},{64,96},{96,128},{128,160},{160,192},{192,224},{224... | collective-permute-start | bytes 860168 | tf_op jit(solution)/shard_map/ppermute | solution.py:20
  29.0 13.7 %all-to-all-start = ((bf16[4,64,1280]{2,1,0:T(8,128)(2,1)}), bf16[4,64,1280]{2,1,0:T(8,128)(2,1)S(1)}, u32[]{:S(2)}, u32[]{:S(2)}) async-start(bf16[4,64,1280]{2,1,0:T(8,128)(2,1)} %reshape.117), calls=%async_computation | async-start | bytes 1310720 | tf_op jit(solution)/shard_map/all_to_all | solution.py:283
  32.5 10.2 %collective-permute-start.9 = (bf16[160,896]{1,0:T(8,128)(2,1)S(1)}, bf16[160,896]{1,0:T(8,128)(2,1)S(1)}, u32[]{:S(2)}, u32[]{:S(2)}) collective-permute-start(bf16[160,896]{1,0:T(8,128)(2,1)S(1)} %collective-permute-done.8.refs_6_), channel_id=1, source_target_pairs={{0,224},{32,0},{64,32},{96,64},{128,96},{160,128},{192,160},{224,1... | collective-permute-start | bytes 860168 | tf_op jit(solution)/shard_map/ppermute | solution.py:20
  35.8 10.2 %collective-permute-start.6 = (bf16[160,896]{1,0:T(8,128)(2,1)}, bf16[160,896]{1,0:T(8,128)(2,1)S(1)}, u32[]{:S(2)}, u32[]{:S(2)}) collective-permute-start(bf16[160,896]{1,0:T(8,128)(2,1)} %collective-permute-done.5.refs_3_), channel_id=1, source_target_pairs={{0,32},{32,64},{64,96},{96,128},{128,160},{160,192},{192,224},{224... | collective-permute-start | bytes 860168 | tf_op jit(solution)/shard_map/ppermute | solution.py:20
  50.6 3.8 %collective-permute-start.10 = (f32[2,64,896]{2,1,0:T(8,128)}, f32[2,64,896]{2,1,0:T(8,128)S(1)}, u32[]{:S(2)}, u32[]{:S(2)}) collective-permute-start(f32[2,64,896]{2,1,0:T(8,128)} %get-tuple-element.18), channel_id=1, source_target_pairs={{0,8},{8,0},{1,9},{9,1},{2,10},{10,2},{3,11},{11,3},{4,12},{12,4},... | collective-permute-start | bytes 1376264 | tf_op jit(solution)/shard_map/ppermute | solution.py:20
  50.6 14.8 %collective-permute-start.19 = (bf16[2048,128]{1,0:T(8,128)(2,1)S(1)}, bf16[2048,128]{1,0:T(8,128)(2,1)S(1)}, u32[]{:S(2)}, u32[]{:S(2)}) collective-permute-start(bf16[2048,128]{1,0:T(8,128)(2,1)S(1)} %bitcast.74), channel_id=1, source_target_pairs={{0,16},{16,0},{1,17},{17,1},{2,18},{18,2},{3,19},{19,3},{4,20},{20... | collective-permute-start | bytes 1572872 | tf_op jit(solution)/shard_map/ppermute | solution.py:20
  52.3 24.3 %collective-permute-start.22 = (bf16[2048,128]{1,0:T(8,128)(2,1)S(1)}, bf16[2048,128]{1,0:T(8,128)(2,1)S(1)}, u32[]{:S(2)}, u32[]{:S(2)}) collective-permute-start(bf16[2048,128]{1,0:T(8,128)(2,1)S(1)} %bitcast.77), channel_id=1, source_target_pairs={{0,16},{16,0},{1,17},{17,1},{2,18},{18,2},{3,19},{19,3},{4,20},{20... | collective-permute-start | bytes 1572872 | tf_op jit(solution)/shard_map/ppermute | solution.py:20
  52.7 32.4 %collective-permute-start.20 = (bf16[2048,128]{1,0:T(8,128)(2,1)S(1)}, bf16[2048,128]{1,0:T(8,128)(2,1)S(1)}, u32[]{:S(2)}, u32[]{:S(2)}) collective-permute-start(bf16[2048,128]{1,0:T(8,128)(2,1)S(1)} %bitcast.75), channel_id=1, source_target_pairs={{0,8},{8,0},{1,9},{9,1},{2,10},{10,2},{3,11},{11,3},{4,12},{12,4},... | collective-permute-start | bytes 1572872 | tf_op jit(solution)/shard_map/ppermute | solution.py:20
  52.7 27.0 %collective-permute-start = (s32[1]{0:T(128)}, s32[1]{0:T(128)}, u32[]{:S(2)}, u32[]{:S(2)}) collective-permute-start(s32[1]{0:T(128)} %param.18), channel_id=1, source_target_pairs={{0,16},{16,0},{1,17},{17,1},{2,18},{18,2},{3,19},{19,3},{4,20},{20... | collective-permute-start | bytes 20 | tf_op jit(solution)/shard_map/ppermute | solution.py:20
  56.2 23.5 %collective-permute-start.11 = (f32[64,640]{1,0:T(8,128)}, f32[64,640]{1,0:T(8,128)S(1)}, u32[]{:S(2)}, u32[]{:S(2)}) collective-permute-start(f32[64,640]{1,0:T(8,128)} %slice.65), channel_id=1, source_target_pairs={{0,16},{16,0},{1,17},{17,1},{2,18},{18,2},{3,19},{19,3},{4,20},{20... | collective-permute-start | bytes 491528 | tf_op jit(solution)/shard_map/ppermute | solution.py:20
  65.4 22.3 %collective-permute-start.23 = (bf16[2048,128]{1,0:T(8,128)(2,1)S(1)}, bf16[2048,128]{1,0:T(8,128)(2,1)S(1)}, u32[]{:S(2)}, u32[]{:S(2)}) collective-permute-start(bf16[2048,128]{1,0:T(8,128)(2,1)S(1)} %bitcast.78), channel_id=1, source_target_pairs={{0,8},{8,0},{1,9},{9,1},{2,10},{10,2},{3,11},{11,3},{4,12},{12,4},... | collective-permute-start | bytes 1572872 | tf_op jit(solution)/shard_map/ppermute | solution.py:20
  76.6 11.0 %collective-permute-start.21 = (bf16[2048,128]{1,0:T(8,128)(2,1)S(1)}, bf16[2048,128]{1,0:T(8,128)(2,1)S(1)}, u32[]{:S(2)}, u32[]{:S(2)}) collective-permute-start(bf16[2048,128]{1,0:T(8,128)(2,1)S(1)} %collective-permute-done.19.refs_1_), channel_id=1, source_target_pairs={{0,8},{8,0},{1,9},{9,1},{2,10},{10,2},{3,11},{11,3},{4,12},{12,4},... | collective-permute-start | bytes 1572872 | tf_op jit(solution)/shard_map/ppermute | solution.py:20
  79.7 8.0 %collective-permute-start.24 = (bf16[2048,128]{1,0:T(8,128)(2,1)S(1)}, bf16[2048,128]{1,0:T(8,128)(2,1)S(1)}, u32[]{:S(2)}, u32[]{:S(2)}) collective-permute-start(bf16[2048,128]{1,0:T(8,128)(2,1)S(1)} %collective-permute-done.22.refs_5_), channel_id=1, source_target_pairs={{0,8},{8,0},{1,9},{9,1},{2,10},{10,2},{3,11},{11,3},{4,12},{12,4},... | collective-permute-start | bytes 1572872 | tf_op jit(solution)/shard_map/ppermute | solution.py:20
  79.7 2.1 collective-permute-start.1
  83.3 14.4 %collective-permute-start.25 = (f32[2,64,256]{2,1,0:T(8,128)S(1)}, f32[2,64,256]{2,1,0:T(8,128)S(1)}, u32[]{:S(2)}, u32[]{:S(2)}) collective-permute-start(f32[2,64,256]{2,1,0:T(8,128)S(1)} %slice.66), channel_id=1, source_target_pairs={{0,16},{16,0},{1,17},{17,1},{2,18},{18,2},{3,19},{19,3},{4,20},{20... | collective-permute-start | bytes 393224 | tf_op jit(solution)/shard_map/ppermute | solution.py:20
  85.1 12.6 %collective-permute-start.12 = (bf16[64,640]{1,0:T(8,128)(2,1)S(1)}, bf16[64,640]{1,0:T(8,128)(2,1)S(1)}, u32[]{:S(2)}, u32[]{:S(2)}) collective-permute-start(bf16[64,640]{1,0:T(8,128)(2,1)S(1)} %multiply_convert_fusion.refs_0_), channel_id=1, source_target_pairs={{0,32},{32,64},{64,96},{96,128},{128,160},{160,192},{192,224},{224... | collective-permute-start | bytes 245768 | tf_op jit(solution)/shard_map/ppermute | solution.py:20
  94.5 5.3 %collective-permute-start.16 = (bf16[64,640]{1,0:T(8,128)(2,1)S(1)}, bf16[64,640]{1,0:T(8,128)(2,1)S(1)}, u32[]{:S(2)}, u32[]{:S(2)}) collective-permute-start(bf16[64,640]{1,0:T(8,128)(2,1)S(1)} %multiply_convert_fusion.refs_0_), channel_id=1, source_target_pairs={{0,224},{32,0},{64,32},{96,64},{128,96},{160,128},{192,160},{224,1... | collective-permute-start | bytes 245768 | tf_op jit(solution)/shard_map/ppermute | solution.py:20
  97.7 5.7 %collective-permute-start.13 = (bf16[64,640]{1,0:T(8,128)(2,1)S(1)}, bf16[64,640]{1,0:T(8,128)(2,1)S(1)}, u32[]{:S(2)}, u32[]{:S(2)}) collective-permute-start(bf16[64,640]{1,0:T(8,128)(2,1)S(1)} %collective-permute-done.12.refs_1_), channel_id=1, source_target_pairs={{0,32},{32,64},{64,96},{96,128},{128,160},{160,192},{192,224},{224... | collective-permute-start | bytes 245768 | tf_op jit(solution)/shard_map/ppermute | solution.py:20
  97.7 11.3 %collective-permute-start.26 = (bf16[128,256]{1,0:T(8,128)(2,1)S(1)}, bf16[128,256]{1,0:T(8,128)(2,1)S(1)}, u32[]{:S(2)}, u32[]{:S(2)}) collective-permute-start(bf16[128,256]{1,0:T(8,128)(2,1)S(1)} %bitcast.80), channel_id=1, source_target_pairs={{0,8},{8,0},{1,9},{9,1},{2,10},{10,2},{3,11},{11,3},{4,12},{12,4},... | collective-permute-start | bytes 196616 | tf_op jit(solution)/shard_map/ppermute | solution.py:20
  99.7 5.7 %collective-permute-start.17 = (bf16[64,640]{1,0:T(8,128)(2,1)S(1)}, bf16[64,640]{1,0:T(8,128)(2,1)S(1)}, u32[]{:S(2)}, u32[]{:S(2)}) collective-permute-start(bf16[64,640]{1,0:T(8,128)(2,1)S(1)} %collective-permute-done.16.refs_7_), channel_id=1, source_target_pairs={{0,224},{32,0},{64,32},{96,64},{128,96},{160,128},{192,160},{224,1... | collective-permute-start | bytes 245768 | tf_op jit(solution)/shard_map/ppermute | solution.py:20
  103.3 5.7 %collective-permute-start.14 = (bf16[64,640]{1,0:T(8,128)(2,1)S(1)}, bf16[64,640]{1,0:T(8,128)(2,1)S(1)}, u32[]{:S(2)}, u32[]{:S(2)}) collective-permute-start(bf16[64,640]{1,0:T(8,128)(2,1)S(1)} %collective-permute-done.13.refs_2_), channel_id=1, source_target_pairs={{0,32},{32,64},{64,96},{96,128},{128,160},{160,192},{192,224},{224... | collective-permute-start | bytes 245768 | tf_op jit(solution)/shard_map/ppermute | solution.py:20
  105.4 5.7 %collective-permute-start.18 = (bf16[64,640]{1,0:T(8,128)(2,1)S(1)}, bf16[64,640]{1,0:T(8,128)(2,1)S(1)}, u32[]{:S(2)}, u32[]{:S(2)}) collective-permute-start(bf16[64,640]{1,0:T(8,128)(2,1)S(1)} %collective-permute-done.17.refs_6_), channel_id=1, source_target_pairs={{0,224},{32,0},{64,32},{96,64},{128,96},{160,128},{192,160},{224,1... | collective-permute-start | bytes 245768 | tf_op jit(solution)/shard_map/ppermute | solution.py:20
  109.0 5.7 %collective-permute-start.15 = (bf16[64,640]{1,0:T(8,128)(2,1)S(1)}, bf16[64,640]{1,0:T(8,128)(2,1)S(1)}, u32[]{:S(2)}, u32[]{:S(2)}) collective-permute-start(bf16[64,640]{1,0:T(8,128)(2,1)S(1)} %collective-permute-done.14.refs_3_), channel_id=1, source_target_pairs={{0,32},{32,64},{64,96},{96,128},{128,160},{160,192},{192,224},{224... | collective-permute-start | bytes 245768 | tf_op jit(solution)/shard_map/ppermute | solution.py:20
  153.1 26.0 %all-to-all-start.1 = ((bf16[8,64,768]{2,1,0:T(8,128)(2,1)}), bf16[8,64,768]{2,1,0:T(8,128)(2,1)S(1)}, u32[]{:S(2)}, u32[]{:S(2)}) async-start(bf16[8,64,768]{2,1,0:T(8,128)(2,1)} %gather_fusion), calls=%async_computation.1 | async-start | bytes 1572864 | tf_op jit(solution)/shard_map/all_to_all | solution.py:315
  159.5 5.8 %collective-permute-start.28 = (bf16[640,160]{0,1:T(8,128)(2,1)S(1)}, bf16[640,160]{0,1:T(8,128)(2,1)S(1)}, u32[]{:S(2)}, u32[]{:S(2)}) collective-permute-start(bf16[640,160]{0,1:T(8,128)(2,1)S(1)} %copy-done.18), channel_id=1, source_target_pairs={{0,16},{16,0},{1,17},{17,1},{2,18},{18,2},{3,19},{19,3},{4,20},{20... | collective-permute-start | bytes 614408 | tf_op jit(solution)/shard_map/ppermute | solution.py:20
  160.0 49.3 %collective-permute-start.27 = (bf16[640,160]{0,1:T(8,128)(2,1)S(1)}, bf16[640,160]{0,1:T(8,128)(2,1)S(1)}, u32[]{:S(2)}, u32[]{:S(2)}) collective-permute-start(bf16[640,160]{0,1:T(8,128)(2,1)S(1)} %copy-done.18), channel_id=1, source_target_pairs={{0,8},{8,0},{1,9},{9,1},{2,10},{10,2},{3,11},{11,3},{4,12},{12,4},... | collective-permute-start | bytes 614408 | tf_op jit(solution)/shard_map/ppermute | solution.py:20
  165.4 43.0 %collective-permute-start.29 = (bf16[640,160]{0,1:T(8,128)(2,1)S(1)}, bf16[640,160]{0,1:T(8,128)(2,1)S(1)}, u32[]{:S(2)}, u32[]{:S(2)}) collective-permute-start(bf16[640,160]{0,1:T(8,128)(2,1)S(1)} %collective-permute-done.28), channel_id=1, source_target_pairs={{0,8},{8,0},{1,9},{9,1},{2,10},{10,2},{3,11},{11,3},{4,12},{12,4},... | collective-permute-start | bytes 614408 | tf_op jit(solution)/shard_map/ppermute | solution.py:20
  212.8 19.3 %all-to-all-start.2 = ((bf16[8,4,64,160]{3,2,1,0:T(8,128)(2,1)}), bf16[8,4,64,160]{3,2,1,0:T(8,128)(2,1)S(1)}, u32[]{:S(2)}, u32[]{:S(2)}) async-start(bf16[8,4,64,160]{3,2,1,0:T(8,128)(2,1)} %copy.15), calls=%async_computation.2 | async-start | bytes 2097152 | tf_op jit(solution)/shard_map/all_to_all | solution.py:322
  (28 other events, 249.3 us)
